TPU v7x, 32 devices: a whole 2x2x4 slice. The times are simulated.
32 devices in a mesh: rows: 8 (over z, y), cols: 4 (over x, core).
Axes of the slice: x: 2, y: 2, z: 4, core: 2. Of those that a mesh axis runs over, the one named last changes fastest.
Arguments:
- coefficients: float32 [4, 1024, 4, 256], P(None, 'rows'), may hold values from -0.03 to 0.09
- support: int32 [4, 1024, 4], P(None, 'rows'), may hold values from 0 to 11, all different within a row
- primal: float32 [12, 256, 256], P('cols'), may hold values from -0.5 to 9, as said below
- dual_inverse: float32 [12, 256, 256], P('cols'), may hold values from -0.5 to 9, as said below
- block_sizes: int32 [12], P('cols'), may hold values from 64 to 256, as said below
- damping: float32 [4, 1024], P(None, 'rows'), may hold values from 0.5 to 2
- right_sides: float32 [4, 32, 1024], P(None, 'cols', 'rows'), may hold values from -6 to 6
Outputs:
- updated: float32 [4, 1024, 4096], P(None, 'rows', 'cols')
- panel_factor: float32 [4, 1024, 128], P(None, 'rows')
- solved: float32 [4, 32, 1024], P(None, 'cols', 'rows')
Inputs may be any that keep to these rules, and one draw needn't show every extreme that they name: `primal`: each block is symmetric positive definite. `dual_inverse`: each block is symmetric positive definite. `block_sizes`: some block has order 256.
All inputs are finite; a program needn't handle non-finite values.
Results may differ from a plain program's by a relative error of at most 0.00015.
Values sent between devices are 32-bit elements; how exact they have to be, the bound alone decides.
A program may use at most 192 MiB of HBM per device.

v0:
```python
import jax
import jax.numpy as jnp
from jax import lax
from jax.sharding import PartitionSpec as P

BS = 256
K = 4
TILE = 128
TPR = 4
highest = lax.Precision.HIGHEST


def broadcast(block, axis, holder):
    block = jnp.where(lax.axis_index(axis) == holder, block, jnp.zeros_like(block))
    return lax.psum(block, axis)


def densify(values, labels, owned_blocks):
    chosen = (labels[..., None] == owned_blocks).astype(jnp.float32)
    return jnp.einsum("tnkq,tnkd->tnqd", chosen, values, precision=highest)


def local(coefficients, support, primal, dual_inverse, block_sizes, damping, right_sides):
    col_index = lax.axis_index("cols")
    row_index = lax.axis_index("rows")
    rows_total = lax.axis_size("rows")
    cols_total = lax.axis_size("cols")
    count_all = TPR * TILE * rows_total
    col_width = count_all // cols_total
    positions = jnp.arange(BS, dtype=jnp.int32)
    active = (positions[None, :] < block_sizes[:, None]).astype(jnp.float32)
    weights = primal * dual_inverse * active[:, :, None] * active[:, None, :]
    every_weight = lax.all_gather(weights, "cols", axis=0, tiled=True)
    all_blocks = jnp.arange(every_weight.shape[0], dtype=jnp.int32)
    own_dense = densify(coefficients, support, all_blocks)
    weighted = jnp.einsum("taqd,qde->taqe", own_dense, every_weight, precision=highest)
    every_coef, every_support = (
        lax.all_gather(coefficients, "rows", axis=1, tiled=True),
        lax.all_gather(support, "rows", axis=1, tiled=True),
    )
    flat_coef = every_coef.reshape(count_all, K, BS)
    flat_support = every_support.reshape(count_all, K)
    column_coef = lax.dynamic_slice_in_dim(flat_coef, col_index * col_width, col_width, 0)
    column_support = lax.dynamic_slice_in_dim(flat_support, col_index * col_width, col_width, 0)
    column_dense = densify(column_coef[None], column_support[None], all_blocks)[0]
    schur_rows = jnp.einsum("taqe,nqe->tan", weighted, column_dense, precision=highest)
    row_global = (jnp.arange(TPR)[:, None] * rows_total + row_index) * TILE + jnp.arange(TILE)[
        None, :
    ]
    col_global = col_index * col_width + jnp.arange(col_width)
    on_diagonal = row_global[:, :, None] == col_global[None, None, :]
    schur_rows = schur_rows + jnp.where(on_diagonal, damping[:, :, None], 0.0)
    corner = broadcast(schur_rows[0, :, :TILE], ("rows", "cols"), 0)
    top_sides = broadcast(right_sides[0], "rows", 0)
    factor = jnp.linalg.cholesky(corner)
    inverse = jax.scipy.linalg.solve_triangular(
        factor, jnp.eye(TILE, dtype=jnp.float32), lower=True
    )
    candidate = jnp.einsum("tak,jk->taj", schur_rows[:, :, :TILE], inverse, precision=highest)
    panel_factor = broadcast(candidate, "cols", 0)
    every_row = lax.all_gather(panel_factor, "rows", axis=1, tiled=True).reshape(count_all, TILE)
    column_panel = lax.dynamic_slice_in_dim(every_row, col_index * col_width, col_width, 0)
    outer_term = jnp.einsum("tak,mk->tam", panel_factor, column_panel, precision=highest)
    row_later = row_global[:, 0] >= TILE
    col_later = col_global >= TILE
    updated = schur_rows - jnp.where(
        row_later[:, None, None] & col_later[None, None, :], outer_term, 0.0
    )
    leading = jnp.dot(top_sides, inverse.T, precision=highest, preferred_element_type=jnp.float32)
    remainder = right_sides - jnp.einsum("sk,tak->tsa", leading, panel_factor, precision=highest)
    solved = jnp.where(row_later[:, None, None], remainder, leading[None, :, :])
    return (updated, panel_factor, solved)


def solution(mesh):
    in_specs = (
        P(None, "rows", None, None),
        P(None, "rows", None),
        P("cols", None, None),
        P("cols", None, None),
        P("cols"),
        P(None, "rows"),
        P(None, "cols", "rows"),
    )
    out_specs = (P(None, "rows", "cols"), P(None, "rows", None), P(None, "cols", "rows"))
    return jax.shard_map(local, mesh=mesh, in_specs=in_specs, out_specs=out_specs, check_vma=False)
```

profile of v0, /device:TPU:0, one launch (start us, length us, event | category | flops | bytes accessed | tf_op | source)
XLA Modules:
  0.0 572.3 jit_solution(2047306640802316005)
XLA Ops:
  7.2 0.0 all-gather.4.cloned.1.call-start
  7.2 0.7 fusion.28
  7.9 0.0 copy-start.3
  7.9 2.4 multiply_multiply_fusion
  10.4 0.0 copy-start.1
  10.4 0.0 all-gather.4.cloned.1.call-update
  10.4 0.0 all-gather.6.cloned.1.call-start
  10.4 0.7 all-gather.6.cloned.1.call-update
  11.1 0.0 all-reduce.3.cloned.1.call-start
  11.2 0.0 copy-done.3
  11.2 0.1 copy.25
  11.4 27.8 %all_gather.13 = s32[4,1024,4]{1,2,0:T(4,128)S(1)} all-gather(s32[4,128,4]{1,2,0:T(4,128)S(1)} %copy-done.3), channel_id=1, replica_groups=mesh['rows'=8,'cols'=4] {'rows'}, dimensions={1}, use_global_device_ids=true | all-gather | bytes 73728 | tf_op jit(solution)/shard_map/all_gather | solution.py:39
  39.2 0.2 copy.28
  39.4 0.1 copy.31
  39.5 0.0 copy-done.1
  39.5 7.4 %fusion.16 = f32[4,128,12,256]{3,2,1,0:T(8,128)} fusion(f32[4,128,4,256]{3,2,1,0:T(4,128)S(1)} %copy-done.1, s32[4,128,4]{2,1,0:T(8,128)S(1)} %copy.25), kind=kOutput, calls=%fused_computation.18 | convolution fusion | flops 75522048 | bytes 8396800 | tf_op jit(solution)/shard_map/tnkq,tnkd->tnqd/dot_general | solution.py:20
  46.9 0.0 all-gather.4.cloned.1.call-done
  46.9 18.5 %fusion.4 = f32[12,256,4,128]{3,1,0,2:T(8,128)} fusion(f32[4,128,12,256]{3,2,1,0:T(8,128)} %fusion.16, f32[12,256,256]{2,1,0:T(8,128)} %all-gather.4.cloned.1.call-done), kind=kOutput, calls=%fused_computation.4 | convolution fusion | flops 4831838208 | bytes 15728640 | tf_op jit(solution)/shard_map/taqd,qde->taqe/dot_general | solution.py:36
  65.4 205.8 %all-gather.6.cloned.1.call-done = f32[4,1024,4,256]{3,2,1,0:T(4,128)} async-done(((f32[4,128,4,256]{3,2,1,0:T(4,128)}), f32[4,1024,4,256]{3,2,1,0:T(4,128)}) %all-gather.6.cloned.1.call-update) | async-done | bytes 16777232 | tf_op jit(solution)/shard_map/all_gather | solution.py:38
  271.3 0.0 copy-start
  271.3 0.0 copy-start.5
  271.3 25.9 %fusion.6 = f32[1024,12,256]{2,1,0:T(8,128)S(1)} fusion(f32[4096,4,256]{2,1,0:T(4,128)} %bitcast.53, s32[]{:T(128)S(6)} %select_n.51, s32[1024,4]{1,0:T(8,128)S(1)} %copy.28), kind=kOutput, calls=%fused_computation.6 | convolution fusion | flops 151044096 | bytes 16793604 | tf_op jit(solution)/shard_map/tnkq,tnkd->tnqd/dot_general | solution.py:20
  297.1 0.0 copy-done
  297.2 0.0 copy-done.5
  297.2 0.0 copy-start.4
  297.2 30.9 %bitcast_add_fusion = f32[4,128,1024]{1,2,0:T(8,128)S(1)} fusion(f32[1024,12,256]{2,1,0:T(8,128)S(1)} %fusion.6, f32[12,256,4,128]{3,1,0,2:T(8,128)S(1)} %copy-done, f32[4,128]{1,0:T(4,128)S(1)} %copy-done.5, s32[4,128]{1,0:T(4,128)S(1)} %copy.31, s32[1024]{0:T(1024)S(1)} %iota_add_fusion.1), kind=kOutput, calls=%fused_computation.9 | convolution fusion | flops 19328925696 | bytes 20979712 | tf_op jit(solution)/shard_map/taqe,nqe->tan/dot_general | solution.py:46
  328.1 0.6 fusion.22
  328.8 0.0 all-reduce.3.cloned.1.call-update
  328.8 0.0 all-reduce.5.cloned.1.call-start
  328.8 117.6 %all-reduce.3.cloned.1.call-done = f32[128,128]{0,1:T(8,128)} async-done(((f32[128,128]{0,1:T(8,128)}), f32[128,128]{0,1:T(8,128)}) %all-reduce.3.cloned.1.call-update) | async-done | bytes 65552 | tf_op jit(solution)/shard_map/psum | solution.py:15
  446.4 0.9 copy.33
  447.4 0.9 fusion.26
  448.2 11.7 %cholesky.16 = f32[128,128]{1,0:T(8,128)S(1)} custom-call(f32[128,128]{1,0:T(8,128)S(1)} %fusion.26), custom_call_target="Cholesky" | custom-call | tf_op jit(solution)/shard_map/jit(cholesky)/cholesky | solution.py:55
  460.0 0.6 compare_reduce_fusion
  460.6 0.7 fusion.21
  461.3 9.8 %custom-call.7 = f32[1,128,128]{1,2,0:T(8,128)S(1)} custom-call(f32[1,128,128]{2,1,0:T(8,128)S(1)} %fusion.21), custom_call_target="InvertDiagBlocksLowerTriangular" | custom-call | tf_op jit(solution)/shard_map/jit(_solve_triangular)/triangular_solve | solution.py:56
  471.1 0.2 fusion.24
  471.4 1.3 convolution_select_fusion
  472.7 0.0 all-reduce.5.cloned.1.call-update
  472.7 0.0 all-gather.8.cloned.1.call-start
  472.7 33.6 %all-reduce.5.cloned.1.call-done = f32[4,128,128]{2,1,0:T(8,128)} async-done(((f32[4,128,128]{2,1,0:T(8,128)}), f32[4,128,128]{2,1,0:T(8,128)}) %all-reduce.5.cloned.1.call-update) | async-done | bytes 262160 | tf_op jit(solution)/shard_map/psum | solution.py:15
  506.4 0.0 all-gather.8.cloned.1.call-update
  506.4 0.0 copy-done.4
  506.4 21.6 %psum.23 = f32[8,128]{1,0:T(8,128)S(1)} all-reduce(f32[8,128]{1,0:T(8,128)S(1)} %select_bitcast_fusion), channel_id=1, replica_groups=mesh['rows'=8,'cols'=4] {'rows'}, use_global_device_ids=true, to_apply=%region_4.5 | all-reduce | flops 1024 | bytes 8192 | tf_op jit(solution)/shard_map/psum | solution.py:15
  528.0 0.1 broadcast_and_fusion
  528.1 0.2 fusion.31
  528.3 1.9 fusion.14
  530.2 27.4 %all-gather.8.cloned.1.call-done = f32[4,1024,128]{2,1,0:T(8,128)} async-done(((f32[4,128,128]{2,1,0:T(8,128)}), f32[4,1024,128]{2,1,0:T(8,128)}) %all-gather.8.cloned.1.call-update) | async-done | bytes 2097168 | tf_op jit(solution)/shard_map/all_gather | solution.py:61
  557.6 4.1 select_subtract_fusion
  561.8 0.0 copy-start.2
  561.8 2.9 copy.36
  564.7 0.0 copy-done.2
  564.7 0.7 copy.54
  (8 shorter events, 0.1 us)
Async XLA Ops:
  7.2 39.7 %all-gather.4.cloned.1.call-start = ((), (), s32[]{:S(2)}) async-start(), calls=%async_computation | async-start | bytes 3932160 | tf_op jit(solution)/shard_map/all_gather | solution.py:33
  7.9 3.3 copy-start.3
  10.4 29.1 %copy-start.1 = (f32[4,128,4,256]{3,2,1,0:T(4,128)S(1)}, f32[4,128,4,256]{3,2,1,0:T(4,128)}, u32[]{:S(2)}) copy-start(f32[4,128,4,256]{3,2,1,0:T(4,128)} %param.7) | copy-start | bytes 6291460
  10.4 260.9 %all-gather.6.cloned.1.call-start = ((), (), s32[]{:S(2)}) async-start(), calls=%async_computation.1 | async-start | bytes 18874368 | tf_op jit(solution)/shard_map/all_gather | solution.py:38
  11.1 435.3 %all-reduce.3.cloned.1.call-start = ((), (), s32[]{:S(2)}) async-start(), calls=%async_computation.2 | async-start | bytes 131072 | tf_op jit(solution)/shard_map/psum | solution.py:15
  271.3 25.9 %copy-start = (f32[12,256,4,128]{3,1,0,2:T(8,128)S(1)}, f32[12,256,4,128]{3,1,0,2:T(8,128)}, u32[]{:S(2)}) copy-start(f32[12,256,4,128]{3,1,0,2:T(8,128)} %fusion.4) | copy-start | bytes 18874372
  271.3 25.9 %copy-start.5 = (f32[4,128]{1,0:T(4,128)S(1)}, f32[4,128]{1,0:T(4,128)}, u32[]{:S(2)}) copy-start(f32[4,128]{1,0:T(4,128)} %param.12) | copy-start | bytes 6148
  297.2 209.2 %copy-start.4 = (f32[4,8,128]{2,1,0:T(8,128)S(1)}, f32[4,8,128]{2,1,0:T(8,128)}, u32[]{:S(2)}) copy-start(f32[4,8,128]{2,1,0:T(8,128)} %param.13) | copy-start | bytes 49156
  328.8 177.6 %all-reduce.5.cloned.1.call-start = ((), (), s32[]{:S(2)}) async-start(), calls=%async_computation.3 | async-start | bytes 524288 | tf_op jit(solution)/shard_map/psum | solution.py:15
  472.7 85.0 %all-gather.8.cloned.1.call-start = ((), (), s32[]{:S(2)}) async-start(), calls=%async_computation.4 | async-start | bytes 2359296 | tf_op jit(solution)/shard_map/all_gather | solution.py:61
  561.8 2.9 copy-start.2
Sparse Core Ops, SparseCore 0:
  10.5 31.2 all-gather.3
  44.0 227.2 all-gather.5
  328.9 117.4 all-reduce.2
  472.8 33.5 all-reduce.4
  508.4 49.1 all-gather.7
where the time goes:
time: 580 us; the launch traced here: 572 us
  waiting for transfers between devices  385 us (66%)
  matrix products  90.5 us (16%)
  blocking collectives  49.4 us (9%)
  other arithmetic  27.6 us (5%)
  between operations  14.3 us (2%)
    all_gather x1, waiting for transfers between devices, local(): lax.all_gather(coefficients, 'rows', axis=1, tiled=True)  206 us
    psum x2, waiting for transfers between devices, broadcast(): return lax.psum(block, axis)  151 us
    dot_general x2, matrix products, densify(): return jnp.einsum('tnkq,tnkd->tnqd', chosen, values, precision=highest)  33.3 us
    dot_general x1, matrix products, local(): jnp.einsum('taqe,nqe->tan', weighted, column_dense, precision=highest)  30.9 us
    all_gather x1, blocking collectives, local(): lax.all_gather(support, 'rows', axis=1, tiled=True)  27.8 us
    all_gather x1, waiting for transfers between devices, local(): lax.all_gather(panel_factor, 'rows', axis=1, tiled=True)  27.4 us
    psum x1, blocking collectives, broadcast(): return lax.psum(block, axis)  21.6 us
    dot_general x1, matrix products, local(): jnp.einsum('taqd,qde->taqe', own_dense, every_weight, precision=highest)  18.5 us
  transfers between devices with their start and end apart: 5, of which 4 were waited for; matrix products, arithmetic and copies ran while one was open for 5% of the time, Pallas kernels for 0%

commit v1 on v0

--- a/solution.py
+++ b/solution.py
@@ -12,7 +12,12 @@
 
 def broadcast(block, axis, holder):
     block = jnp.where(lax.axis_index(axis) == holder, block, jnp.zeros_like(block))
-    return lax.psum(block, axis)
+
+    def list_layers_all(x_part):
+        v_next = lax.all_gather(x_part, axis_name=axis).sum(axis=0)
+        return v_next
+
+    return list_layers_all(block)
 
 
 def densify(values, labels, owned_blocks):

time: 580 us -> 489 us (0.84); the launches traced: 572 us -> 489 us
  waiting for transfers between devices: 385 us -> 293 us
  blocking collectives: 49.4 us -> 58.6 us
    psum x2 -> x0, waiting for transfers between devices: 151 us -> none  [broadcast(): return lax.psum(block, axis)]
    all_gather x0 -> x2, waiting for transfers between devices: none -> 69.9 us  [list_layers_all(): v_next = lax.all_gather(x_part, axis_name=axis).sum(axis=0)]
    all_gather x0 -> x1, blocking collectives: none -> 30.8 us  [list_layers_all(): v_next = lax.all_gather(x_part, axis_name=axis).sum(axis=0)]
    psum x1 -> x0, blocking collectives: 21.6 us -> none  [broadcast(): return lax.psum(block, axis)]
    dot_general x1, matrix products: 30.9 us -> 45.9 us  [local(): jnp.einsum('taqe,nqe->tan', weighted, column_dense, precision=highest)]
    dot_general x2, matrix products: 33.3 us -> 19.5 us  [densify(): return jnp.einsum('tnkq,tnkd->tnqd', chosen, values, precision=highest)]
    all_gather x1, waiting for transfers between devices: 27.4 us -> 16.7 us  [local(): lax.all_gather(panel_factor, 'rows', axis=1, tiled=True)]
  transfers between devices with their start and end apart: 5 -> 5, of which waited for: 4 -> 4; matrix products, arithmetic and copies ran while one was open for 5% -> 6% of each run, Pallas kernels for 0% -> 0%
where the time goes in v1:
time: 489 us
  waiting for transfers between devices  293 us (60%)
  matrix products  91.7 us (19%)
  blocking collectives  58.6 us (12%)
  other arithmetic  30.5 us (6%)
  between operations  13.9 us (3%)
    all_gather x1, waiting for transfers between devices, local(): lax.all_gather(coefficients, 'rows', axis=1, tiled=True)  206 us
    all_gather x2, waiting for transfers between devices, list_layers_all(): v_next = lax.all_gather(x_part, axis_name=axis).sum(axis=0)  69.9 us
    dot_general x1, matrix products, local(): jnp.einsum('taqe,nqe->tan', weighted, column_dense, precision=highest)  45.9 us
    all_gather x1, blocking collectives, list_layers_all(): v_next = lax.all_gather(x_part, axis_name=axis).sum(axis=0)  30.8 us
    all_gather x1, blocking collectives, local(): lax.all_gather(support, 'rows', axis=1, tiled=True)  27.8 us
    dot_general x2, matrix products, densify(): return jnp.einsum('tnkq,tnkd->tnqd', chosen, values, precision=highest)  19.5 us
    dot_general x1, matrix products, local(): jnp.einsum('taqd,qde->taqe', own_dense, every_weight, precision=highest)  18.5 us
    all_gather x1, waiting for transfers between devices, local(): lax.all_gather(panel_factor, 'rows', axis=1, tiled=True)  16.7 us
  transfers between devices with their start and end apart: 5, of which 4 were waited for; matrix products, arithmetic and copies ran while one was open for 6% of the time, Pallas kernels for 0%

profile of v1, /device:TPU:0, one launch (start us, length us, event | category | flops | bytes accessed | tf_op | source)
XLA Modules:
  0.0 488.9 jit_solution(17123197717625786480)
XLA Ops:
  7.2 0.0 all-gather.7.cloned.1.call-start
  7.2 0.7 fusion.27
  7.9 0.0 copy-start.2
  7.9 2.4 multiply_multiply_fusion
  10.4 0.0 copy-start.1
  10.4 0.0 all-gather.7.cloned.1.call-update
  10.4 0.0 all-gather.9.cloned.1.call-start
  10.4 0.7 all-gather.9.cloned.1.call-update
  11.1 0.0 all-gather.11.cloned.1.call-start
  11.2 0.0 copy-done.2
  11.2 0.1 copy.17
  11.4 27.8 %all_gather.27 = s32[4,1024,4]{1,2,0:T(4,128)S(1)} all-gather(s32[4,128,4]{1,2,0:T(4,128)S(1)} %copy-done.2), channel_id=1, replica_groups=mesh['rows'=8,'cols'=4] {'rows'}, dimensions={1}, use_global_device_ids=true | all-gather | bytes 73728 | tf_op jit(solution)/shard_map/all_gather | solution.py:44
  39.2 0.2 copy.20
  39.4 0.1 copy.23
  39.5 0.0 copy-done.1
  39.5 7.4 %fusion.16 = f32[4,128,12,256]{3,2,1,0:T(8,128)} fusion(f32[4,128,4,256]{3,2,1,0:T(4,128)S(1)} %copy-done.1, s32[4,128,4]{2,1,0:T(8,128)S(1)} %copy.17), kind=kOutput, calls=%fused_computation.18 | convolution fusion | flops 75522048 | bytes 8396800 | tf_op jit(solution)/shard_map/tnkq,tnkd->tnqd/dot_general | solution.py:25
  46.9 0.0 all-gather.7.cloned.1.call-done
  46.9 18.5 %fusion.4 = f32[12,256,4,128]{3,1,0,2:T(8,128)} fusion(f32[4,128,12,256]{3,2,1,0:T(8,128)} %fusion.16, f32[12,256,256]{2,1,0:T(8,128)} %all-gather.7.cloned.1.call-done), kind=kOutput, calls=%fused_computation.4 | convolution fusion | flops 4831838208 | bytes 15728640 | tf_op jit(solution)/shard_map/taqd,qde->taqe/dot_general | solution.py:41
  65.4 205.8 %all-gather.9.cloned.1.call-done = f32[4,1024,4,256]{3,2,1,0:T(4,128)} async-done(((f32[4,128,4,256]{3,2,1,0:T(4,128)}), f32[4,1024,4,256]{3,2,1,0:T(4,128)}) %all-gather.9.cloned.1.call-update) | async-done | bytes 16777232 | tf_op jit(solution)/shard_map/all_gather | solution.py:43
  271.3 0.0 copy-start
  271.3 0.0 copy-start.4
  271.3 12.0 %fusion.6 = f32[1024,12,256]{2,1,0:T(8,128)S(1)} fusion(f32[4096,4,256]{2,1,0:T(4,128)} %bitcast.52, s32[]{:T(128)S(6)} %select_n.47, s32[1024,4]{1,0:T(8,128)S(1)} %copy.20), kind=kOutput, calls=%fused_computation.6 | convolution fusion | flops 151044096 | bytes 16793604 | tf_op jit(solution)/shard_map/tnkq,tnkd->tnqd/dot_general | solution.py:25
  283.3 0.0 copy-done
  283.3 0.0 copy-done.4
  283.3 45.9 %bitcast_add_fusion = f32[4,128,1024]{2,1,0:T(8,128)S(1)} fusion(f32[1024,12,256]{2,1,0:T(8,128)S(1)} %fusion.6, f32[12,256,4,128]{3,1,0,2:T(8,128)S(1)} %copy-done, f32[4,128]{1,0:T(4,128)S(1)} %copy-done.4, s32[1024]{0:T(1024)S(1)} %iota_add_fusion.1, s32[4,128]{1,0:T(4,128)S(1)} %copy.23), kind=kOutput, calls=%fused_computation.9 | convolution fusion | flops 19328925696 | bytes 20979712 | tf_op jit(solution)/shard_map/taqe,nqe->tan/dot_general | solution.py:51
  329.3 0.6 slice_select_fusion
  329.9 0.0 all-gather.11.cloned.1.call-update
  330.0 0.3 all-gather.15.cloned.1.call-start
  330.2 0.0 copy-start.3
  330.3 54.2 %all-gather.11.cloned.1.call-done = f32[32,128,128]{2,1,0:T(8,128)} async-done(((f32[1,128,128]{2,1,0:T(8,128)}), f32[32,128,128]{2,1,0:T(8,128)}) %all-gather.11.cloned.1.call-update) | async-done | bytes 2097168 | tf_op jit(solution)/shard_map/all_gather | solution.py:17
  384.5 1.7 reduce_sum.27
  386.2 0.1 copy.24
  386.3 11.7 %cholesky.16 = f32[128,128]{1,0:T(8,128)S(1)} custom-call(f32[128,128]{1,0:T(8,128)S(1)} %fusion.25), custom_call_target="Cholesky" | custom-call | tf_op jit(solution)/shard_map/jit(cholesky)/cholesky | solution.py:60
  398.1 0.6 compare_reduce_fusion
  398.7 0.7 fusion.21
  399.4 9.8 %custom-call.7 = f32[1,128,128]{1,2,0:T(8,128)S(1)} custom-call(f32[1,128,128]{2,1,0:T(8,128)S(1)} %fusion.21), custom_call_target="InvertDiagBlocksLowerTriangular" | custom-call | tf_op jit(solution)/shard_map/jit(_solve_triangular)/triangular_solve | solution.py:61
  409.2 0.2 fusion.23
  409.4 1.1 convolution_select_fusion
  410.5 0.0 all-gather.15.cloned.1.call-update
  410.5 0.0 all-gather.13.cloned.1.call-start
  410.6 15.6 %all-gather.15.cloned.1.call-done = f32[16,128,128]{2,1,0:T(8,128)} async-done(((f32[4,128,128]{2,1,0:T(8,128)}), f32[16,128,128]{2,1,0:T(8,128)}) %all-gather.15.cloned.1.call-update) | async-done | bytes 1048592 | tf_op jit(solution)/shard_map/all_gather | solution.py:17
  426.2 2.0 reduce_sum.28
  428.3 0.0 all-gather.13.cloned.1.call-update
  428.3 0.0 copy-done.3
  428.3 30.8 %all_gather.33 = f32[8,8,128]{2,1,0:T(8,128)S(1)} all-gather(f32[1,8,128]{2,1,0:T(8,128)S(1)} %slice_select_fusion.1), channel_id=1, replica_groups=mesh['rows'=8,'cols'=4] {'rows'}, dimensions={0}, use_global_device_ids=true | all-gather | bytes 36864 | tf_op jit(solution)/shard_map/all_gather | solution.py:17
  459.1 0.1 broadcast_and_fusion
  459.2 0.2 fusion.30
  459.4 1.9 fusion.14
  461.3 16.7 %all-gather.13.cloned.1.call-done = f32[4,1024,128]{2,1,0:T(8,128)} async-done(((f32[4,128,128]{2,1,0:T(8,128)}), f32[4,1024,128]{2,1,0:T(8,128)}) %all-gather.13.cloned.1.call-update) | async-done | bytes 2097168 | tf_op jit(solution)/shard_map/all_gather | solution.py:66
  478.0 4.3 select_subtract_fusion
  (10 shorter events, 0.1 us)
Async XLA Ops:
  7.2 39.7 %all-gather.7.cloned.1.call-start = ((), (), s32[]{:S(2)}) async-start(), calls=%async_computation | async-start | bytes 3932160 | tf_op jit(solution)/shard_map/all_gather | solution.py:38
  7.9 3.3 copy-start.2
  10.4 29.1 %copy-start.1 = (f32[4,128,4,256]{3,2,1,0:T(4,128)S(1)}, f32[4,128,4,256]{3,2,1,0:T(4,128)}, u32[]{:S(2)}) copy-start(f32[4,128,4,256]{3,2,1,0:T(4,128)} %param.7) | copy-start | bytes 6291460
  10.4 260.9 %all-gather.9.cloned.1.call-start = ((), (), s32[]{:S(2)}) async-start(), calls=%async_computation.1 | async-start | bytes 18874368 | tf_op jit(solution)/shard_map/all_gather | solution.py:43
  11.1 373.3 %all-gather.11.cloned.1.call-start = ((), (), s32[]{:S(2)}) async-start(), calls=%async_computation.2 | async-start | bytes 2162688 | tf_op jit(solution)/shard_map/all_gather | solution.py:17
  271.3 12.1 %copy-start = (f32[12,256,4,128]{3,1,0,2:T(8,128)S(1)}, f32[12,256,4,128]{3,1,0,2:T(8,128)}, u32[]{:S(2)}) copy-start(f32[12,256,4,128]{3,1,0,2:T(8,128)} %fusion.4) | copy-start | bytes 18874372
  271.3 12.1 %copy-start.4 = (f32[4,128]{1,0:T(4,128)S(1)}, f32[4,128]{1,0:T(4,128)}, u32[]{:S(2)}) copy-start(f32[4,128]{1,0:T(4,128)} %param.12) | copy-start | bytes 6148
  330.0 96.3 %all-gather.15.cloned.1.call-start = ((), (), s32[]{:S(2)}) async-start(), calls=%async_computation.4 | async-start | bytes 1310720 | tf_op jit(solution)/shard_map/all_gather | solution.py:17
  330.2 98.0 %copy-start.3 = (f32[4,8,128]{2,1,0:T(8,128)S(1)}, f32[4,8,128]{2,1,0:T(8,128)}, u32[]{:S(2)}) copy-start(f32[4,8,128]{2,1,0:T(8,128)} %param.13) | copy-start | bytes 49156
  410.5 67.5 %all-gather.13.cloned.1.call-start = ((), (), s32[]{:S(2)}) async-start(), calls=%async_computation.3 | async-start | bytes 2359296 | tf_op jit(solution)/shard_map/all_gather | solution.py:66
Sparse Core Ops, SparseCore 0:
  10.5 31.2 all-gather.6
  44.0 227.2 all-gather.8
  330.1 54.3 all-gather.10
  410.7 15.5 all-gather.14
  428.9 49.1 all-gather.12
